TPU v7x, 32 devices: a whole 2x2x4 slice. The times are simulated.
32 devices in a mesh: ia: 2 (over y), ja: 4 (over x, core), ka: 4 (over z).
Axes of the slice: x: 2, y: 2, z: 4, core: 2. Of those that a mesh axis runs over, the one named last changes fastest.
Arguments:
- tensor: float32 [32, 256, 8192], P('ia', 'ka', 'ja'), may hold values from -6 to 6
- factor_b: float32 [8192, 64], P(('ja', 'ka')), may hold values from -1 to 1
- factor_c: float32 [256, 64], P('ka'), may hold values from -1 to 1
Outputs:
- factor_a: float32 [32, 64], P(('ia', 'ja', 'ka'))
- mode_two: float32 [64, 4, 2048], P(None, 'ja', ('ia', 'ka'))
All inputs are finite; a program needn't handle non-finite values.
Results may differ from a plain program's by a relative error of at most 0.00026.
Values sent between devices are 32-bit elements; how exact they have to be, the bound alone decides.
No kernel may reach another device: no remote copies, remote signals or barrier semaphores. Data moves between devices by JAX's collectives and lax.ppermute only.
A program may use at most 64 MiB of HBM per device.

v0:
```python
import jax
import jax.numpy as jnp
from jax import lax
from jax.sharding import PartitionSpec as P


def body(tensor, factor_b, factor_c):
    highest = lax.Precision.HIGHEST
    factor_rank = factor_c.shape[1]
    row_block = tensor.shape[0]
    column_block = tensor.shape[2]
    local_b = jnp.dot(factor_b.T, factor_b, precision=highest, preferred_element_type=jnp.float32)
    local_c = jnp.dot(factor_c.T, factor_c, precision=highest, preferred_element_type=jnp.float32)
    gram_b = lax.psum(local_b, ("ja", "ka"))
    gram_c = lax.psum(local_c, "ka")
    triangle = jnp.linalg.cholesky(gram_b * gram_c)
    partial_value = jnp.einsum("ikj,kr->rij", tensor, factor_c, precision=highest)
    mode_one = jnp.einsum(
        "rij,jr->ir",
        partial_value,
        lax.all_gather(factor_b, "ka", axis=0, tiled=True),
        precision=highest,
    )
    empty_two = jnp.zeros((factor_rank, column_block), jnp.float32)
    full_sum = lax.psum(mode_one, ("ja", "ka"))
    a_block = jax.scipy.linalg.cho_solve((triangle, True), full_sum.T).T
    row_count = row_block // (lax.axis_size("ja") * lax.axis_size("ka"))
    offset = (lax.axis_index("ja") * lax.axis_size("ka") + lax.axis_index("ka")) * row_count
    a_rows = lax.dynamic_slice_in_dim(a_block, offset, row_count, 0)
    contracted = jnp.einsum("ikj,kr->rij", tensor, factor_c, precision=highest)
    mode_partial = empty_two + jnp.einsum("rij,ir->rj", contracted, a_block, precision=highest)
    reduced = lax.psum_scatter(mode_partial, ("ia", "ka"), scatter_dimension=1, tiled=True)
    return (a_rows, reduced.reshape(factor_rank, 1, reduced.shape[1]))


def solution(mesh):
    placed = (P("ia", "ka", "ja"), P(("ja", "ka"), None), P("ka", None))
    return jax.shard_map(
        body,
        mesh=mesh,
        in_specs=placed,
        out_specs=(P(("ia", "ja", "ka"), None), P(None, "ja", ("ia", "ka"))),
        check_vma=False,
    )
```

profile of v0, /device:TPU:0, one launch (start us, length us, event | category | flops | bytes accessed | tf_op | source)
XLA Modules:
  0.0 229.5 jit_solution(2462762528005702529)
XLA Ops:
  7.2 0.0 copy-start
  7.2 0.0 reduce-scatter.2.cloned.1.call-start
  7.2 17.6 %all_gather.3 = f32[2048,64]{0,1:T(8,128)S(1)} all-gather(f32[512,64]{0,1:T(8,128)} %param.4), channel_id=1, replica_groups=mesh['ia'=2,'ja'=4,'ka'=4] {'ka'}, dimensions={0}, use_global_device_ids=true | all-gather | bytes 655360 | tf_op jit(solution)/shard_map/all_gather | solution.py:21
  24.8 1.2 fusion.13
  26.1 0.0 copy-done
  26.1 0.2 fusion.14
  26.3 11.6 %fusion.6 = f32[64,16,2048]{2,0,1:T(8,128)} fusion(f32[16,64,2048]{2,1,0:T(8,128)} %param.3, f32[64,64]{1,0:T(8,128)S(1)} %copy-done), kind=kOutput, calls=%fused_computation.8 | convolution fusion | flops 1610612736 | bytes 16793600 | tf_op jit(solution)/shard_map/ikj,kr->rij/dot_general | solution.py:17
  37.9 19.8 %psum.22 = f32[64,64]{0,1:T(8,128)S(1)} all-reduce(f32[64,64]{0,1:T(8,128)S(1)} %fusion.14), channel_id=1, replica_groups=mesh['ia'=2,'ja'=4,'ka'=4] {'ka'}, use_global_device_ids=true, to_apply=%region_1.0 | all-reduce | flops 4096 | bytes 32768 | tf_op jit(solution)/shard_map/psum | solution.py:15
  57.7 17.9 %fusion.2 = f32[64,1,16]{2,1,0:T(1,128)S(1)} fusion(f32[64,16,2048]{2,0,1:T(8,128)} %fusion.6, f32[2048,64,1]{0,1,2:T(8,128)S(1)} %bitcast.31), kind=kOutput, calls=%fused_computation.2 | convolution fusion | flops 25165824 | bytes 8916992 | tf_op jit(solution)/shard_map/rij,jr->ir/dot_general | solution.py:18
  75.6 58.2 %all-reduce = (f32[16,64]{0,1:T(8,128)S(1)}, f32[64,64]{0,1:T(8,128)S(1)}) all-reduce(f32[16,64]{0,1:T(8,128)S(1)} %bitcast.33, f32[64,64]{0,1:T(8,128)S(1)} %fusion.13), channel_id=1, replica_groups=mesh['ia'=2,'ja'=4,'ka'=4] {'ja','ka'}, use_global_device_ids=true, to_apply=%region_4.5 | all-reduce | flops 5120 | bytes 40960 | tf_op jit(solution)/shard_map/psum | solution.py:25
  133.8 0.1 copy.7
  133.9 5.8 %cholesky.16 = f32[64,64]{1,0:T(8,128)S(1)} custom-call(f32[64,64]{1,0:T(8,128)S(1)} %fusion.12), custom_call_target="Cholesky" | custom-call | tf_op jit(solution)/shard_map/jit(cholesky)/cholesky | solution.py:16
  139.7 0.6 compare_reduce_fusion
  140.4 0.7 fusion.5
  141.0 4.9 %custom-call.10 = f32[1,64,64]{1,2,0:T(8,128)S(1)} custom-call(f32[1,64,64]{2,1,0:T(8,128)S(1)} %fusion.5), custom_call_target="InvertDiagBlocksLowerTriangular" | custom-call | tf_op jit(solution)/shard_map/jit(_cho_solve)/triangular_solve | solution.py:26
  145.9 0.3 fusion.10
  146.2 0.2 fusion.8
  146.4 0.1 copy.15
  146.5 12.3 %fusion = f32[64,1,2048]{2,1,0:T(1,128)S(1)} fusion(f32[16,64,1]{0,2,1:T(1,128)S(1)} %copy.15, f32[64,16,2048]{2,0,1:T(8,128)} %fusion.6), kind=kOutput, calls=%fused_computation | convolution fusion | flops 25165824 | bytes 8916992 | tf_op jit(solution)/shard_map/rij,ir->rj/dot_general | solution.py:31
  158.8 1.0 copy.25
  159.8 0.0 reduce-scatter.2.cloned.1.call-update
  159.8 0.5 constant_dynamic-slice_fusion
  160.3 60.9 %reduce-scatter.2.cloned.1.call-done = f32[64,256]{1,0:T(8,128)} async-done(((f32[64,2048]{1,0:T(8,128)}), f32[64,256]{1,0:T(8,128)}) %reduce-scatter.2.cloned.1.call-update) | async-done | bytes 65552 | tf_op jit(solution)/shard_map/reduce_scatter | solution.py:32
  221.2 1.5 reshape.20
  (3 shorter events, 0.0 us)
Async XLA Ops:
  7.2 18.9 %copy-start = (f32[64,64]{1,0:T(8,128)S(1)}, f32[64,64]{1,0:T(8,128)}, u32[]{:S(2)}) copy-start(f32[64,64]{1,0:T(8,128)} %param.5) | copy-start | bytes 49156
  7.2 214.0 %reduce-scatter.2.cloned.1.call-start = ((), (), s32[]{:S(2)}) async-start(), calls=%async_computation.1 | async-start | bytes 589824 | tf_op jit(solution)/shard_map/reduce_scatter | solution.py:32
Sparse Core Ops, SparseCore 0:
  159.9 61.2 reduce-scatter.1
where the time goes:
time: 230 us
  blocking collectives  95.6 us (42%)
  waiting for transfers between devices  60.9 us (26%)
  matrix products  43.7 us (19%)
  between operations  14.1 us (6%)
  other arithmetic  12.1 us (5%)
  local copies, waits for them, and re-layouts  3.15 us (1%)
    reduce_scatter x1, waiting for transfers between devices, body(): lax.psum_scatter(mode_partial, ('ia', 'ka'), scatter_dimension=1, tiled=T...  60.9 us
    psum x1, blocking collectives, body(): full_sum = lax.psum(mode_one, ('ja', 'ka'))  58.2 us
    psum x1, blocking collectives, body(): gram_c = lax.psum(local_c, 'ka')  19.8 us
    dot_general x1, matrix products, body(): jnp.einsum('rij,jr->ir', partial_value, lax.all_gather(factor_b, 'ka', ax...  17.9 us
    all_gather x1, blocking collectives, body(): lax.all_gather(factor_b, 'ka', axis=0, tiled=True)  17.6 us
    dot_general x1, matrix products, body(): jnp.einsum('rij,ir->rj', contracted, a_block, precision=highest)  12.3 us
    dot_general x1, matrix products, body(): jnp.einsum('ikj,kr->rij', tensor, factor_c, precision=highest)  11.6 us
    another operation x3, other arithmetic, body(): triangle = jnp.linalg.cholesky(gram_b * gram_c)  6.52 us
  transfers between devices with their start and end apart: 1, of which 1 were waited for; matrix products, arithmetic and copies ran while one was open for 0% of the time, Pallas kernels for 0%

commit v1 on v0

--- a/solution.py
+++ b/solution.py
@@ -22,7 +22,7 @@
         precision=highest,
     )
     empty_two = jnp.zeros((factor_rank, column_block), jnp.float32)
-    full_sum = lax.psum(mode_one, ("ja", "ka"))
+    full_sum = lax.psum(lax.psum(mode_one, "ka"), "ja")
     a_block = jax.scipy.linalg.cho_solve((triangle, True), full_sum.T).T
     row_count = row_block // (lax.axis_size("ja") * lax.axis_size("ka"))
     offset = (lax.axis_index("ja") * lax.axis_size("ka") + lax.axis_index("ka")) * row_count

time: 230 us -> 240 us (1.043)
  blocking collectives: 95.6 us -> 105 us
    psum x2 -> x3, blocking collectives: 78 us -> 87 us  [the longest x1 59.9 us: body(): gram_b = lax.psum(local_b, ('ja', 'ka'))]
where the time goes in v1:
time: 240 us
  blocking collectives  105 us (44%)
  waiting for transfers between devices  62.2 us (26%)
  matrix products  43.7 us (18%)
  between operations  14.1 us (6%)
  other arithmetic  12.1 us (5%)
  local copies, waits for them, and re-layouts  3.15 us (1%)
    reduce_scatter x1, waiting for transfers between devices, body(): lax.psum_scatter(mode_partial, ('ia', 'ka'), scatter_dimension=1, tiled=T...  62.2 us
    psum x1, blocking collectives, body(): gram_b = lax.psum(local_b, ('ja', 'ka'))  59.9 us
    psum x2, blocking collectives, body(): full_sum = lax.psum(lax.psum(mode_one, 'ka'), 'ja')  27 us
    dot_general x1, matrix products, body(): jnp.einsum('rij,jr->ir', partial_value, lax.all_gather(factor_b, 'ka', ax...  17.9 us
    all_gather x1, blocking collectives, body(): lax.all_gather(factor_b, 'ka', axis=0, tiled=True)  17.6 us
    dot_general x1, matrix products, body(): jnp.einsum('rij,ir->rj', contracted, a_block, precision=highest)  12.3 us
    dot_general x1, matrix products, body(): jnp.einsum('ikj,kr->rij', tensor, factor_c, precision=highest)  11.6 us
    another operation x3, other arithmetic, body(): triangle = jnp.linalg.cholesky(gram_b * gram_c)  6.52 us
  transfers between devices with their start and end apart: 1, of which 1 were waited for; matrix products, arithmetic and copies ran while one was open for 0% of the time, Pallas kernels for 0%

profile of v1, /device:TPU:0, one launch (start us, length us, event | category | flops | bytes accessed | tf_op | source)
XLA Modules:
  0.0 239.9 jit_solution(10543073811703003133)
XLA Ops:
  7.2 0.0 copy-start
  7.2 0.0 reduce-scatter.2.cloned.1.call-start
  7.2 17.6 %all_gather.3 = f32[2048,64]{0,1:T(8,128)S(1)} all-gather(f32[512,64]{0,1:T(8,128)} %param.4), channel_id=1, replica_groups=mesh['ia'=2,'ja'=4,'ka'=4] {'ka'}, dimensions={0}, use_global_device_ids=true | all-gather | bytes 655360 | tf_op jit(solution)/shard_map/all_gather | solution.py:21
  24.8 1.2 fusion.13
  26.1 0.2 fusion.14
  26.3 11.6 %fusion.6 = f32[64,16,2048]{2,0,1:T(8,128)} fusion(f32[16,64,2048]{2,1,0:T(8,128)} %param.3, f32[64,64]{1,0:T(8,128)S(1)} %copy-done), kind=kOutput, calls=%fused_computation.8 | convolution fusion | flops 1610612736 | bytes 16793600 | tf_op jit(solution)/shard_map/ikj,kr->rij/dot_general | solution.py:17
  37.9 59.9 %psum.28 = f32[64,64]{0,1:T(8,128)S(1)} all-reduce(f32[64,64]{0,1:T(8,128)S(1)} %fusion.13), channel_id=1, replica_groups=mesh['ia'=2,'ja'=4,'ka'=4] {'ja','ka'}, use_global_device_ids=true, to_apply=%region_0.0 | all-reduce | flops 4096 | bytes 32768 | tf_op jit(solution)/shard_map/psum | solution.py:14
  97.8 17.9 %fusion.2 = f32[64,1,16]{2,1,0:T(1,128)S(1)} fusion(f32[64,16,2048]{2,0,1:T(8,128)} %fusion.6, f32[2048,64,1]{0,1,2:T(8,128)S(1)} %bitcast.31), kind=kOutput, calls=%fused_computation.2 | convolution fusion | flops 25165824 | bytes 8916992 | tf_op jit(solution)/shard_map/rij,jr->ir/dot_general | solution.py:18
  115.7 16.8 %all-reduce = (f32[16,64]{0,1:T(8,128)S(1)}, f32[64,64]{0,1:T(8,128)S(1)}) all-reduce(f32[16,64]{0,1:T(8,128)S(1)} %bitcast.33, f32[64,64]{0,1:T(8,128)S(1)} %fusion.14), channel_id=1, replica_groups=mesh['ia'=2,'ja'=4,'ka'=4] {'ka'}, use_global_device_ids=true, to_apply=%region_4.5 | all-reduce | flops 5120 | bytes 40960 | tf_op jit(solution)/shard_map/psum | solution.py:25
  132.5 0.1 copy.7
  132.6 5.8 %cholesky.16 = f32[64,64]{1,0:T(8,128)S(1)} custom-call(f32[64,64]{1,0:T(8,128)S(1)} %fusion.12), custom_call_target="Cholesky" | custom-call | tf_op jit(solution)/shard_map/jit(cholesky)/cholesky | solution.py:16
  138.5 0.6 compare_reduce_fusion
  139.1 0.7 fusion.5
  139.8 4.9 %custom-call.10 = f32[1,64,64]{1,2,0:T(8,128)S(1)} custom-call(f32[1,64,64]{2,1,0:T(8,128)S(1)} %fusion.5), custom_call_target="InvertDiagBlocksLowerTriangular" | custom-call | tf_op jit(solution)/shard_map/jit(_cho_solve)/triangular_solve | solution.py:26
  144.7 10.3 %psum.31 = f32[16,64]{0,1:T(8,128)S(1)} all-reduce(f32[16,64]{0,1:T(8,128)S(1)} %get-tuple-element.2), channel_id=1, replica_groups=mesh['ia'=2,'ja'=4,'ka'=4] {'ja'}, use_global_device_ids=true, to_apply=%region_5.6 | all-reduce | flops 1024 | bytes 8192 | tf_op jit(solution)/shard_map/psum | solution.py:25
  154.9 0.2 fusion.10
  155.2 0.2 fusion.8
  155.4 0.1 copy.15
  155.5 12.3 %fusion = f32[64,1,2048]{2,1,0:T(1,128)S(1)} fusion(f32[16,64,1]{0,2,1:T(1,128)S(1)} %copy.15, f32[64,16,2048]{2,0,1:T(8,128)} %fusion.6), kind=kOutput, calls=%fused_computation | convolution fusion | flops 25165824 | bytes 8916992 | tf_op jit(solution)/shard_map/rij,ir->rj/dot_general | solution.py:31
  167.8 1.0 copy.25
  168.8 0.0 reduce-scatter.2.cloned.1.call-update
  168.8 0.5 constant_dynamic-slice_fusion
  169.3 62.2 %reduce-scatter.2.cloned.1.call-done = f32[64,256]{1,0:T(8,128)} async-done(((f32[64,2048]{1,0:T(8,128)}), f32[64,256]{1,0:T(8,128)}) %reduce-scatter.2.cloned.1.call-update) | async-done | bytes 65552 | tf_op jit(solution)/shard_map/reduce_scatter | solution.py:32
  231.5 1.5 reshape.20
  (4 shorter events, 0.0 us)
Async XLA Ops:
  7.2 18.9 %copy-start = (f32[64,64]{1,0:T(8,128)S(1)}, f32[64,64]{1,0:T(8,128)}, u32[]{:S(2)}) copy-start(f32[64,64]{1,0:T(8,128)} %param.5) | copy-start | bytes 49156
  7.2 224.4 %reduce-scatter.2.cloned.1.call-start = ((), (), s32[]{:S(2)}) async-start(), calls=%async_computation.1 | async-start | bytes 589824 | tf_op jit(solution)/shard_map/reduce_scatter | solution.py:32
Sparse Core Ops, SparseCore 0:
  168.9 62.5 reduce-scatter.1
